TPU v7x, 512 devices: a whole 4x4x16 slice. The times are simulated.
512 devices in a mesh: ex: 128 (over y, x, z_lo), tok: 4 (over z_hi, core).
Axes of the slice: x: 4, y: 4, z: 16 (z_hi: 2, z_lo: 8; z = z_hi * 8 + z_lo), core: 2. Of those that a mesh axis runs over, the one named last changes fastest.
Arguments:
- proj_rows: bfloat16 [1048576, 128], P(('ex', 'tok')), may hold values from -6 to 6
- query_features: bfloat16 [8192, 4096], P('ex'), may hold values from -0.09375 to 0.09375
- doc_lengths: int32 [128, 32], P('ex'), may hold values from 1 to 4096, 8192 in all within a row
- owner_map: int32 [128, 32], P('ex'), may hold values from 0 to 31, each once within a row
Outputs:
- scores: float32 [8192, 4096], P('ex', 'tok')
Inputs may be any that keep to these rules, and one draw needn't show every extreme that they name: `owner_map`: each row lists the slots 0 to 31 once each. `doc_lengths`: each row sums to 8192; its largest entry is exactly 4096.
All inputs are finite; a program needn't handle non-finite values.
Results may differ from a plain program's by a relative error of at most 0.0029.
Values may be sent and summed in bfloat16 or wider, within the bound.
A program may use at most 64 MiB of HBM per device.

v0:
```python
import jax
import jax.numpy as jnp
from jax import lax
from jax.sharding import PartitionSpec as P


def slot_lookup(lengths, owner_slots, positions):
    doc_ends = jnp.cumsum(lengths)
    doc_index = jnp.sum((positions[:, None] >= doc_ends[None, :]).astype(jnp.int32), axis=1)
    doc_match = doc_index[:, None] == jnp.arange(lengths.shape[0], dtype=jnp.int32)[None, :]
    return jnp.sum(jnp.where(doc_match, owner_slots[None, :], 0), axis=1)


def kron_sums(row_data, slots, targets):
    proj_width = row_data.shape[1] // 2
    count = row_data.shape[0]
    input_rows = row_data[:, :proj_width]
    grad_rows = row_data[:, proj_width:]

    def slot_group(slot_set):
        slot_mask = (slots[:, None] == slot_set[None, :]).astype(jnp.bfloat16)
        spread = (slot_mask[:, :, None] * grad_rows[:, None, :]).reshape(count, 4 * proj_width)
        return jnp.einsum("ta,tb->ab", spread, input_rows, preferred_element_type=jnp.float32)

    result = lax.map(slot_group, targets.reshape(-1, 4))
    return result.reshape(targets.shape[0], proj_width * proj_width)


def body(proj_rows, query_features, doc_lengths, owner_map):
    lengths = doc_lengths[0]
    owner_slots = owner_map[0]
    tok_count = lax.axis_size("tok")
    doc_dev = owner_slots.shape[0] // tok_count
    tok_index = lax.axis_index("tok")
    targets = tok_index * doc_dev + jnp.arange(doc_dev, dtype=jnp.int32)
    portion = lax.all_gather(proj_rows, "tok", axis=0, tiled=True)
    positions = jnp.arange(portion.shape[0], dtype=jnp.int32)
    summed = kron_sums(portion, slot_lookup(lengths, owner_slots, positions), targets)
    own_lengths = jnp.sum(
        jnp.where(owner_slots[None, :] == targets[:, None], lengths[None, :], 0), axis=1
    )
    features = (summed / jnp.sqrt(own_lengths.astype(jnp.float32))[:, None]).astype(jnp.bfloat16)
    return jnp.einsum(
        "qf,df->qd",
        query_features,
        lax.all_gather(features, "ex", axis=0, tiled=True),
        preferred_element_type=jnp.float32,
    )


def solution(mesh):
    placed = (P(("ex", "tok"), None), P("ex", None), P("ex", None), P("ex", None))
    return jax.shard_map(
        body, mesh=mesh, in_specs=placed, out_specs=P("ex", "tok"), check_vma=False
    )
```

profile of v0, /device:TPU:0, one launch (start us, length us, event | category | flops | bytes accessed | tf_op | source)
XLA Modules:
  0.0 1094.7 jit_solution(13539632485198462072)
XLA Ops:
  6.5 0.0 copy-start
  6.5 0.0 all-gather.3.cloned.1.call-start
  6.5 0.7 all-gather.3.cloned.1.call-update
  7.3 0.0 all-gather.5.cloned.1.call-start
  7.3 0.7 copy.9
  8.1 0.1 reduce-window.8
  8.1 0.1 reduce
  8.3 0.9 select_reduce_fusion.1
  9.1 0.2 convert_reduce_fusion
  9.3 0.9 select_reduce_fusion
  10.3 74.3 %all-gather.3.cloned.1.call-done = bf16[8192,128]{1,0:T(8,128)(2,1)} async-done(((bf16[2048,128]{1,0:T(8,128)(2,1)}), bf16[8192,128]{1,0:T(8,128)(2,1)}) %all-gather.3.cloned.1.call-update) | async-done | bytes 2097168 | tf_op jit(solution)/shard_map/all_gather | solution.py:36
  84.5 4.3 fusion.2
  88.8 2.7 copy.10
  91.5 6.2 while.10
  91.5 0.1 compare_convert_fusion.2
  91.6 1.6 broadcast_multiply_fusion.2
  93.2 1.4 fusion.14
  94.6 0.1 compare_convert_fusion.2
  94.7 1.6 broadcast_multiply_fusion.2
  96.3 1.4 fusion.14
  97.7 0.1 copy.11
  97.9 0.1 reshape.75
  98.0 0.7 divide_convert_fusion
  98.7 0.0 all-gather.5.cloned.1.call-update
  98.7 982.3 %all-gather.5.cloned.1.call-done = bf16[1024,4096]{1,0:T(8,128)(2,1)} async-done(((bf16[8,4096]{1,0:T(8,128)(2,1)}), bf16[1024,4096]{1,0:T(8,128)(2,1)}) %all-gather.5.cloned.1.call-update) | async-done | bytes 8388624 | tf_op jit(solution)/shard_map/all_gather | solution.py:46
  1081.1 0.0 copy-done
  1081.1 6.7 convolution_bitcast_fusion.1
  (6 shorter events, 0.0 us)
Async XLA Ops:
  6.5 1074.5 %copy-start = (bf16[64,4096]{1,0:T(8,128)(2,1)S(1)}, bf16[64,4096]{1,0:T(8,128)(2,1)}, u32[]{:S(2)}) copy-start(bf16[64,4096]{1,0:T(8,128)(2,1)} %param.7) | copy-start | bytes 1572868
  6.5 78.0 %all-gather.3.cloned.1.call-start = ((), (), s32[]{:S(2)}) async-start(), calls=%async_computation | async-start | bytes 2621440 | tf_op jit(solution)/shard_map/all_gather | solution.py:36
  7.3 1073.8 %all-gather.5.cloned.1.call-start = ((), (), s32[]{:S(2)}) async-start(), calls=%async_computation.1 | async-start | bytes 8454144 | tf_op jit(solution)/shard_map/all_gather | solution.py:46
Sparse Core Ops, SparseCore 0:
  9.5 75.0 all-gather.2
  98.9 982.1 all-gather.4
where the time goes:
time: 1090 us
  waiting for transfers between devices  1060 us (97%)
  between operations  13.5 us (1%)
    all_gather x1, waiting for transfers between devices, body(): lax.all_gather(features, 'ex', axis=0, tiled=True)  982 us
    all_gather x1, waiting for transfers between devices, body(): portion = lax.all_gather(proj_rows, 'tok', axis=0, tiled=True)  74.3 us
  transfers between devices with their start and end apart: 2, of which 2 were waited for; matrix products, arithmetic and copies ran while one was open for 0% of the time, Pallas kernels for 0%

commit v1 on v0

--- a/solution.py
+++ b/solution.py
@@ -40,11 +40,17 @@
         jnp.where(owner_slots[None, :] == targets[:, None], lengths[None, :], 0), axis=1
     )
     features = (summed / jnp.sqrt(own_lengths.astype(jnp.float32))[:, None]).astype(jnp.bfloat16)
+
+    def _run_run(vector):
+        column = []
+        for _ in range(jax.lax.axis_size("ex")):
+            column.append(vector)
+        spare = jnp.stack(column)
+        block_next = jax.lax.all_to_all(spare, axis_name="ex", split_axis=0, concat_axis=0)
+        return jnp.concatenate(block_next, 0)
+
     return jnp.einsum(
-        "qf,df->qd",
-        query_features,
-        lax.all_gather(features, "ex", axis=0, tiled=True),
-        preferred_element_type=jnp.float32,
+        "qf,df->qd", query_features, _run_run(features), preferred_element_type=jnp.float32
     )
 
 

time: 1090 us -> 494 us (0.45)
  waiting for transfers between devices: 1060 us -> 75 us
  blocking collectives: 0 us -> 379 us
    all_gather x1 -> x0, waiting for transfers between devices: 982 us -> none  [body(): lax.all_gather(features, 'ex', axis=0, tiled=True)]
    all_to_all x0 -> x1, blocking collectives: none -> 379 us  [_run_run(): jax.lax.all_to_all(spare, axis_name='ex', split_axis=0, concat_axis=0)]
  transfers between devices with their start and end apart: 2 -> 1, of which waited for: 2 -> 1; matrix products, arithmetic and copies ran while one was open for 0% -> 1% of each run, Pallas kernels for 0% -> 0%
where the time goes in v1:
time: 494 us; the launch traced here: 488 us
  blocking collectives  379 us (77%)
  waiting for transfers between devices  75 us (15%)
  between operations  13.5 us (3%)
  local copies, waits for them, and re-layouts  8.97 us (2%)
  matrix products  6.25 us (1%)
  other arithmetic  5.57 us (1%)
    all_to_all x1, blocking collectives, _run_run(): jax.lax.all_to_all(spare, axis_name='ex', split_axis=0, concat_axis=0)  379 us
    all_gather x1, waiting for transfers between devices, body(): portion = lax.all_gather(proj_rows, 'tok', axis=0, tiled=True)  74.3 us
  transfers between devices with their start and end apart: 1, of which 1 were waited for; matrix products, arithmetic and copies ran while one was open for 1% of the time, Pallas kernels for 0%

profile of v1, /device:TPU:0, one launch (start us, length us, event | category | flops | bytes accessed | tf_op | source)
XLA Modules:
  0.0 488.5 jit_solution(7045535031229497827)
XLA Ops:
  6.5 0.0 copy-start
  6.5 0.0 all-gather.2.cloned.1.call-start
  6.5 0.7 all-gather.2.cloned.1.call-update
  7.3 0.7 copy.9
  8.0 0.1 reduce-window.8
  8.1 0.1 reduce
  8.2 0.9 select_reduce_fusion.1
  9.1 0.2 convert_reduce_fusion
  9.3 0.9 select_reduce_fusion
  10.2 74.3 %all-gather.2.cloned.1.call-done = bf16[8192,128]{1,0:T(8,128)(2,1)} async-done(((bf16[2048,128]{1,0:T(8,128)(2,1)}), bf16[8192,128]{1,0:T(8,128)(2,1)}) %all-gather.2.cloned.1.call-update) | async-done | bytes 2097168 | tf_op jit(solution)/shard_map/all_gather | solution.py:36
  84.5 4.3 fusion.7
  88.8 2.7 copy.10
  91.5 6.2 %while.10 = (s32[]{:T(128)}, f32[2,256,64]{1,2,0:T(8,128)S(1)}, s32[8192]{0:T(1024)S(1)}, s32[2,4]{1,0:T(2,128)S(1)}, bf16[8192,64]{0,1:T(8,128)(2,1)}, /*index=5*/bf16[8192,64]{1,0:T(8,128)(2,1)S(1)}, s32[]{:T(128)}) while((s32[]{:T(128)}, f32[2,256,64]{1,2,0:T(8,128)S(1)}, s32[8192]{0:T(1024)S(1)}, s32[2,4]{1,0:T(2,128)S(1)}, ...), condition=%wide.region_4.5_spmd, body=%wide.region_3.4_spmd.sunk | while | flops 270598144 | bytes 11763853 | solution.py:25
  91.5 0.1 compare_convert_fusion.2
  91.6 1.6 broadcast_multiply_fusion.2
  93.2 1.4 fusion.18
  94.6 0.1 compare_convert_fusion.2
  94.7 1.6 broadcast_multiply_fusion.2
  96.3 1.4 fusion.18
  97.7 0.1 copy.11
  97.9 0.1 reshape.87
  98.0 0.1 divide_convert_fusion
  98.1 1.0 stack.2
  99.1 379.2 %all_to_all.5 = bf16[128,8,4096]{2,1,0:T(8,128)(2,1)S(1)} all-to-all(bf16[128,8,4096]{2,1,0:T(8,128)(2,1)S(1)} %stack.2), channel_id=1, replica_groups=mesh['ex'=128,'tok'=4] {'ex'}, dimensions={0} | all-to-all | bytes 16777216 | tf_op jit(solution)/shard_map/all_to_all | solution.py:49
  478.3 0.0 copy-done
  478.3 3.4 fusion.4
  (6 shorter events, 0.0 us)
Async XLA Ops:
  6.5 471.7 %copy-start = (bf16[64,4096]{1,0:T(8,128)(2,1)S(1)}, bf16[64,4096]{1,0:T(8,128)(2,1)}, u32[]{:S(2)}) copy-start(bf16[64,4096]{1,0:T(8,128)(2,1)} %param.7) | copy-start | bytes 1572868
  6.5 78.0 %all-gather.2.cloned.1.call-start = ((), (), s32[]{:S(2)}) async-start(), calls=%async_computation.1 | async-start | bytes 2621440 | tf_op jit(solution)/shard_map/all_gather | solution.py:36
Sparse Core Ops, SparseCore 0:
  9.5 75.0 all-gather.1
